TPU v7x, 32 devices: a whole 2x2x4 slice. The times are simulated.
32 devices in a mesh: mem: 4 (over z), slab: 8 (over y, x, core).
Axes of the slice: x: 2, y: 2, z: 4, core: 2. Of those that a mesh axis runs over, the one named last changes fastest.
Arguments:
- ensemble: float32 [256, 256, 128], P('mem', 'slab'), may hold values from -6 to 6
- diffusivity: float32 [256, 128], P('slab'), may hold values from 0.15 to 0.25
- velocity: float32 [2, 256, 128], P(None, 'slab'), may hold values from -0.5 to 0.5
- obs_value: float32 [40960], P(('mem', 'slab')), may hold values from -6 to 6
- obs_weight: float32 [40960], P(('mem', 'slab')), may hold values from 0.3 to 12
- obs_slab: int32 [40960, 1], P(('mem', 'slab')), may hold values from 0 to 7; in each aligned block of 1280 rows (0 to 1279, 1280 to 2559, ...) at most 320 rows name the same one
- obs_cell: int32 [40960], P(('mem', 'slab')), may hold values from 0 to 1023
Outputs:
- analysis: float32 [256, 256, 128], P('mem', 'slab')
Inputs may be any that keep to these rules, and one draw needn't show every extreme that they name: `obs_slab`: among the 1280 observations stored on one device, no slab is named more than 320 times; on some device one slab is named exactly 320 times.
All inputs are finite; a program needn't handle non-finite values.
Results may differ from a plain program's by a relative error of at most 0.0085.
Values sent between devices are 32-bit elements; how exact they have to be, the bound alone decides.
No kernel may reach another device: no remote copies, remote signals or barrier semaphores. Data moves between devices by JAX's collectives and lax.ppermute only.
A program may use at most 128 MiB of HBM per device.

v0:
```python
import functools

import jax
import jax.numpy as jnp
from jax import lax
from jax.experimental import pallas as pl
from jax.experimental.pallas import tpu as pltpu
from jax.sharding import PartitionSpec as P


STEPS = 4
NS_STEPS = 5
HALF = 4
SUB = 8
F32 = jnp.float32
BF16 = jnp.bfloat16


VMEM = pl.BlockSpec(memory_space=pltpu.VMEM)
SMEM = pl.BlockSpec(memory_space=pltpu.SMEM)
HBM = pl.BlockSpec(memory_space=pl.ANY)
PARAMS = pltpu.CompilerParams(vmem_limit_bytes=16 << 20)


def near(arrays):
    return [pltpu.with_memory_space_constraint(a, pltpu.VMEM) for a in arrays]


def far(arrays):
    return [pltpu.with_memory_space_constraint(a, pltpu.HBM) for a in arrays]


def put_table(table, row, diffuse, drift_x, drift_y):
    width = diffuse.shape[-1]
    parts = (
        1.0 - 4.0 * diffuse,
        diffuse - 0.5 * drift_x,
        diffuse + 0.5 * drift_x,
        diffuse + 0.5 * drift_y,
        diffuse - 0.5 * drift_y,
    )
    for k, part in enumerate(parts):
        for r in range(part.shape[0]):
            table[row + r, k] = jnp.broadcast_to(part[r : r + 1], (SUB, width))


def advance(field, scratch, table, first, count):
    members, width = field.shape[1:]
    source = field
    for step in range(STEPS):
        target = scratch[step % 2]
        for i in range(first + step + 1, first + count - step - 1):
            coef = [table[i, k] for k in range(5)]
            for m in range(0, members, SUB):
                at = pl.ds(m, SUB)
                center = source[i, at, :]
                target[i, at, :] = (
                    (center * coef[0] + pltpu.roll(center, width - 1, 1) * coef[1])
                    + (pltpu.roll(center, 1, 1) * coef[2] + source[i - 1, at, :] * coef[3])
                    + source[i + 1, at, :] * coef[4]
                )
        source = target
    return source


def inner_kernel(n_mem, *refs):
    place, ens_hbm, diffuse_hbm, drift_hbm = refs[:4]
    edges, early, late = refs[4:6], refs[6 : 6 + n_mem], refs[6 + n_mem : 6 + 2 * n_mem]
    field, table, ping, pong, ens_ref, diffuse_ref, drift_ref, sems = refs[6 + 2 * n_mem :]
    rows, width = diffuse_ref.shape
    members = ens_hbm.shape[0]

    copies = [
        pltpu.make_async_copy(diffuse_hbm, diffuse_ref, sems.at[n_mem]),
        pltpu.make_async_copy(drift_hbm, drift_ref, sems.at[n_mem + 1]),
    ]
    for g in range(n_mem):
        copies.append(
            pltpu.make_async_copy(ens_hbm.at[:, pl.ds(g * SUB, SUB)], ens_ref.at[g], sems.at[g])
        )
    for copy in copies:
        copy.start()
    copies[0].wait()
    copies[1].wait()
    put_table(table, 0, diffuse_ref[...], drift_ref[0], drift_ref[1])
    for g in range(n_mem):
        copies[2 + g].wait()
        group = ens_ref.at[g].reshape(members * SUB, width)
        for r in range(SUB):
            field[g * SUB + r] = group[pl.ds(r, members, stride=SUB), :]
    for edge, first in zip(edges, (0, rows - STEPS)):
        for r in range(STEPS):
            row = first + r
            edge[r, :members, :] = field[row]
            edge[r, members : members + 1, :] = diffuse_ref[row : row + 1, :]
            for k in range(2):
                edge[r, members + 1 + k : members + 2 + k, :] = drift_ref[k, row : row + 1, :]

    done = advance(field, (ping, pong), table, 0, rows)
    for shift in range(n_mem):
        group = lax.rem(place[0] + shift, n_mem)
        top = group * SUB + jnp.where(group == 0, HALF, 0)
        bottom = jnp.minimum(group * SUB + HALF, rows - 2 * HALF)
        for r in range(HALF):
            early[shift][r] = done[top + r]
            late[shift][r] = done[bottom + r]


def inner(n_mem, place, ens, diffusivity, velocity):
    rows, width = diffusivity.shape
    members = ens.shape[0]
    part = pltpu.VMEM((HALF, members, width), F32)
    edge = pltpu.VMEM((STEPS, members + SUB, width), F32)
    shapes = [edge] * 2 + [part] * (2 * n_mem)
    outs = pl.pallas_call(
        functools.partial(inner_kernel, n_mem),
        in_specs=[SMEM] + [HBM] * 3,
        out_specs=[VMEM] * len(shapes),
        out_shape=shapes,
        scratch_shapes=[
            pltpu.VMEM((rows, members, width), F32),
            pltpu.VMEM((rows, 5, SUB, width), F32),
            pltpu.VMEM((rows, members, width), F32),
            pltpu.VMEM((rows, members, width), F32),
            pltpu.VMEM((n_mem, members, SUB, width), F32),
            pltpu.VMEM(diffusivity.shape, F32),
            pltpu.VMEM(velocity.shape, F32),
            pltpu.SemaphoreType.DMA((n_mem + 2,)),
        ],
        compiler_params=PARAMS,
        name="inner",
    )(place, *far([ens, diffusivity, velocity]))
    return outs[:2], outs[2 : 2 + n_mem], outs[2 + n_mem :]


def outer_kernel(n_mem, *refs):
    place, top_ref, bottom_ref, diffuse_ref, drift_ref, above, below = refs[:7]
    outs = refs[7 + n_mem : 7 + 2 * n_mem]
    field, table, ping, pong = refs[7 + 2 * n_mem :]
    rows = diffuse_ref.shape[0]
    members = field.shape[1]
    span = 3 * STEPS
    lows = (0, rows - 2 * STEPS)

    for side, ref in enumerate((top_ref, bottom_ref)):
        halo = (above, below)[side]
        inside = side * span + (1 - side) * STEPS
        outside = side * span + side * 2 * STEPS
        part = ref.reshape(members * SUB, ref.shape[-1])
        for r in range(SUB):
            field[inside + r] = part[pl.ds(r, members, stride=SUB), :]
        rows_at = pl.ds(lows[side], SUB)
        put_table(table, inside, diffuse_ref[rows_at], drift_ref[0, rows_at], drift_ref[1, rows_at])
        for r in range(STEPS):
            field[outside + r] = halo[r, :members, :]
            put_table(
                table, outside + r, *(halo[r, members + k : members + k + 1, :] for k in range(3))
            )
        done = advance(field, (ping, pong), table, side * span, span)

    for shift in range(n_mem):
        group = lax.rem(place[0] + shift, n_mem)

        @pl.when((group == 0) | (group == n_mem - 1))
        def _(group=group, shift=shift):
            start = jnp.where(group == 0, 0, span) + STEPS
            for r in range(HALF):
                outs[shift][r] = done[start + r]


def outer(n_mem, place, ens, diffusivity, velocity, halos, late):
    rows, width = diffusivity.shape
    members = ens.shape[0]
    span = 6 * STEPS
    late = near(late)
    block = (members, SUB, width)
    whole = [pl.BlockSpec(a.shape, lambda i, n=a.ndim: (0,) * n) for a in (diffusivity, velocity)]
    return pl.pallas_call(
        functools.partial(outer_kernel, n_mem),
        grid=(1,),
        in_specs=[
            SMEM,
            pl.BlockSpec(block, lambda i: (0, 0, 0)),
            pl.BlockSpec(block, lambda i: (0, rows // SUB - 1, 0)),
        ]
        + whole
        + [VMEM] * (2 + n_mem),
        out_specs=[VMEM] * n_mem,
        out_shape=[pltpu.VMEM(a.shape, F32) for a in late],
        scratch_shapes=[
            pltpu.VMEM((span, members, width), F32),
            pltpu.VMEM((span, 5, SUB, width), F32),
            pltpu.VMEM((span, members, width), F32),
            pltpu.VMEM((span, members, width), F32),
        ],
        input_output_aliases={7 + k: k for k in range(n_mem)},
        compiler_params=PARAMS,
        name="outer",
    )(place, ens, ens, diffusivity, velocity, *near(halos), *late)


def tally_kernel(*refs):
    out_ref, sems, value_ref, weight_ref, slab_ref, cell_ref = refs[4:]
    copies = [pltpu.make_async_copy(refs[k], refs[6 + k], sems.at[k]) for k in range(4)]
    for copy in copies:
        copy.start()
    for copy in copies:
        copy.wait()
    lanes = out_ref.shape[-1]
    blocks = value_ref.shape[0]
    n_slab = out_ref.shape[0]
    width = out_ref.shape[-1]
    bins = n_slab * SUB
    bin_id = lax.broadcasted_iota(jnp.int32, (bins, lanes), 0)
    column_id = lax.broadcasted_iota(jnp.int32, (width, lanes), 0)
    totals = jnp.zeros((2 * bins, width), F32)
    for b in range(blocks):
        cell = cell_ref[b : b + 1, :]
        weight = weight_ref[b : b + 1, :]
        product = weight * value_ref[b : b + 1, :]
        named = slab_ref[:, pl.ds(b * lanes, lanes)] * SUB + cell // width
        here = bin_id == named
        column = jnp.where(column_id == cell % width, 1.0, 0.0).astype(BF16)
        rest = jnp.concatenate(
            [jnp.where(here, weight, 0.0), jnp.where(here, product, 0.0)], axis=0
        )
        for _ in range(3):
            piece = rest.astype(BF16)
            rest = rest - piece.astype(F32)
            totals = totals + lax.dot_general(
                piece, column, (((1,), (1,)), ((), ())), preferred_element_type=F32
            )
    for k in range(2 * n_slab):
        out_ref[k % n_slab, k // n_slab] = totals[k * SUB : (k + 1) * SUB]


def tally(value, weight, slab, cell, n_slab, width):
    value, weight, cell = (a.reshape(-1, width) for a in (value, weight, cell))
    arrays = [value, weight, slab.reshape(1, -1), cell]
    return pl.pallas_call(
        tally_kernel,
        in_specs=[HBM] * 4,
        out_specs=VMEM,
        out_shape=pltpu.VMEM((n_slab, 2, SUB, width), F32),
        scratch_shapes=[pltpu.SemaphoreType.DMA((4,))]
        + [pltpu.VMEM(a.shape, a.dtype) for a in arrays],
        compiler_params=PARAMS,
        name="tally",
    )(*far(arrays))


def halves(a):
    high = a.astype(BF16)
    return high, (a - high.astype(F32)).astype(BF16)


def left(a):
    return jnp.concatenate(halves(a), axis=1)


def right(b):
    both = jnp.concatenate(halves(b), axis=1)
    return jnp.concatenate([both, both], axis=0)


def product(a, b):
    both = jnp.dot(a, b, preferred_element_type=F32)
    width = both.shape[1] // 2
    return both[:, :width] + both[:, width:]


def analyse_kernel(chunk, n_mem, place, tallies_ref, *refs):
    fields, outs, spread = refs[:n_mem], refs[n_mem : 2 * n_mem], refs[2 * n_mem]
    local, width = fields[0].shape[1:]
    members = n_mem * local
    n_slab = tallies_ref.shape[0]
    eye = lax.broadcasted_iota(jnp.int32, (width, width), 0) == lax.broadcasted_iota(
        jnp.int32, (width, width), 1
    )
    total = tallies_ref[0]
    for k in range(1, n_slab):
        total = total + tallies_ref[k]
    first_half = (place[0] == 0) if chunk else (place[0] != 0)
    total = jnp.where(first_half, total[:, :HALF], total[:, HALF:])
    patches = range(HALF)

    means, grams, iterates, scales, gaps = [], [], [], [], []
    for p in patches:
        weight = total[0, p : p + 1, :]
        mean = sum(jnp.sum(f[p], axis=0, keepdims=True) for f in fields) * (1.0 / members)
        for k, f in enumerate(fields):
            spread[p, k * local : (k + 1) * local, :] = (f[p] - mean).astype(BF16)
        s = spread[p]
        gram = lax.dot_general(s, s, (((0,), (0,)), ((), ())), preferred_element_type=F32)
        scaled = gram * weight
        trace = jnp.sum(jnp.where(eye, scaled, 0.0), keepdims=True)
        square = jnp.sum(scaled * scaled.T, keepdims=True)
        norm = (members - 1.0) ** 2 * members + 2.0 * (members - 1.0) * trace + square
        scale = 8.0 * jnp.sqrt(norm * (1.0 / members))
        inverse = 1.0 / scale
        iterates.append(scaled * inverse + jnp.where(eye, (members - 1.0) * inverse, 0.0))
        means.append(mean)
        grams.append(gram)
        scales.append(inverse)
        gaps.append(total[1, p : p + 1, :] - weight * mean)

    roots = [None] * HALF
    for step in range(NS_STEPS):
        last = step == NS_STEPS - 1
        if step == 0:
            both = iterates
        else:
            rights = [right(y) for y in iterates]
            both = [product(left(roots[p]), rights[p]) for p in patches]
        factors = [jnp.where(eye, 1.5, 0.0) - 0.5 * b for b in both]
        lefts = [left(f) for f in factors]
        if not last:
            iterates = [
                product(lefts[p], right(iterates[p]) if step == 0 else rights[p]) for p in patches
            ]
        if step == 0:
            roots = factors
        else:
            roots = [product(lefts[p], right(roots[p])) for p in patches]

    for p in patches:
        root = right(roots[p])
        line = jnp.broadcast_to(gaps[p], (SUB, width))
        line = product(left(line), root)
        line = product(left(line), root)
        line = product(left(line), right(grams[p]))
        base = means[p] + line[:1] * scales[p]
        transform = (jnp.sqrt((members - 1.0) * scales[p]) * roots[p]).astype(BF16)
        update = lax.dot_general(
            spread[p], transform, (((1,), (1,)), ((), ())), preferred_element_type=F32
        )
        for k, out in enumerate(outs):
            out[pl.ds(p, local, stride=HALF), :] = base + update[k * local : (k + 1) * local]


def analyse(chunk, n_mem, place, tallies, fields):
    local, width = fields[0].shape[1:]
    shape = pltpu.VMEM((local * HALF, width), F32)
    return pl.pallas_call(
        functools.partial(analyse_kernel, chunk, n_mem),
        in_specs=[SMEM] + [VMEM] * (1 + n_mem),
        out_specs=[VMEM] * n_mem,
        out_shape=[shape] * n_mem,
        scratch_shapes=[pltpu.VMEM((HALF, n_mem * local, width), BF16)],
        compiler_params=PARAMS,
    )(place, *near([tallies, *fields]))


def settle_kernel(chunk, n_mem, place, *refs):
    parts, out_ref, sems = refs[:n_mem], refs[-2], refs[-1]
    copies = []
    for shift in range(n_mem):
        group = lax.rem(place[0] + shift, n_mem)
        second = (group != 0) if chunk else (group == 0)
        at = 2 * group + second.astype(jnp.int32)
        copies.append(pltpu.make_async_copy(parts[shift], out_ref.at[:, at], sems.at[shift]))
    for copy in copies:
        copy.start()
    for copy in copies:
        copy.wait()


def settle(chunk, n_mem, place, parts, out=None):
    local, width = parts[0].shape[0] // HALF, parts[0].shape[1]
    parts = near([a.reshape(local, HALF, width) for a in parts])
    return pl.pallas_call(
        functools.partial(settle_kernel, chunk, n_mem),
        in_specs=[SMEM] + [VMEM] * n_mem + [HBM] * chunk,
        out_specs=HBM,
        out_shape=jax.ShapeDtypeStruct((local, 2 * n_mem, HALF, width), F32),
        scratch_shapes=[pltpu.SemaphoreType.DMA((n_mem,))],
        input_output_aliases={1 + n_mem: 0} if chunk else {},
        compiler_params=PARAMS,
    )(place, *parts, *([out] if chunk else []))


def shards(ensemble, diffusivity, velocity, obs_value, obs_weight, obs_slab, obs_cell):
    n_slab, n_mem = lax.axis_size("slab"), lax.axis_size("mem")
    members, rows, width = ensemble.shape
    place = lax.axis_index("mem").reshape(1)
    assert rows == n_mem * SUB
    up = [(i, (i + 1) % n_slab) for i in range(n_slab)]
    down = [(j, i) for i, j in up]

    def send(parts, sign):
        moved = [parts[0]]
        for shift in range(1, n_mem):
            ways = [(i, (i + sign * shift) % n_mem) for i in range(n_mem)]
            moved.append(lax.ppermute(parts[shift], "mem", ways))
        return moved

    (head, tail), early, late = inner(n_mem, place, ensemble, diffusivity, velocity)
    early = send(early, 1)
    above = lax.ppermute(tail, "slab", up)
    below = lax.ppermute(head, "slab", down)
    counts = tally(obs_value, obs_weight, obs_slab, obs_cell, n_slab, width)
    counts = lax.all_to_all(counts, "slab", split_axis=0, concat_axis=0, tiled=True)
    late = outer(n_mem, place, ensemble, diffusivity, velocity, (above, below), late)
    late = send(late, 1)
    early = send(analyse(0, n_mem, place, counts, early), -1)
    late = send(analyse(1, n_mem, place, counts, late), -1)
    out = settle(0, n_mem, place, early)
    return settle(1, n_mem, place, late, out).reshape(members, rows, width)


def solution(mesh):
    return jax.shard_map(
        shards,
        mesh=mesh,
        in_specs=(
            P("mem", "slab", None),
            P("slab", None),
            P(None, "slab", None),
            P(("mem", "slab")),
            P(("mem", "slab")),
            P(("mem", "slab"), None),
            P(("mem", "slab")),
        ),
        out_specs=P("mem", "slab", None),
        check_vma=False,
    )
```

profile of v0, /device:TPU:0, one launch (start us, length us, event | category | flops | bytes accessed | tf_op | source)
XLA Modules:
  0.0 59.0 jit_solution(555924157793802660)
XLA Ops:
  0.0 0.0 copy-start
  0.0 3.5 %inner.1 = (f32[4,72,128]{2,1,0:T(8,128)S(1)}, f32[4,72,128]{2,1,0:T(8,128)S(1)}, f32[4,64,128]{2,1,0:T(8,128)S(1)}, f32[4,64,128]{2,1,0:T(8,128)S(1)}, f32[4,64...) custom-call(s32[1]{0:T(128)} %bitcast.refs_0_.place, ...), custom_call_target="tpu_custom_call" | custom-call | tf_op jit(solution)/shard_map/inner/pallas_call | solution.py:115
  3.5 0.5 collective-permute-start
  4.1 2.9 %collective-permute-start.1 = (f32[4,72,128]{2,1,0:T(8,128)S(1)}, f32[4,72,128]{2,1,0:T(8,128)S(1)}, u32[]{:S(2)}, u32[]{:S(2)}) collective-permute-start(f32[4,72,128]{2,1,0:T(8,128)S(1)} %get-tuple-element.28), channel_id=1, source_target_pairs={{1,0},{2,1},{3,2},{4,3},{5,4},{6,5},{7,6},{0,7},{9,8},{10,9},{11,1... | collective-permute-start | bytes 442376 | tf_op jit(solution)/shard_map/ppermute | solution.py:400
  7.0 2.3 %collective-permute-start.8 = (f32[4,64,128]{2,1,0:T(8,128)S(1)}, f32[4,64,128]{2,1,0:T(8,128)S(1)}, u32[]{:S(2)}, u32[]{:S(2)}) collective-permute-start(f32[4,64,128]{2,1,0:T(8,128)S(1)} %get-tuple-element.42), channel_id=1, source_target_pairs={{0,8},{8,16},{16,24},{24,0},{1,9},{9,17},{17,25},{25,1},{2,10},{10... | collective-permute-start | bytes 393224 | tf_op jit(solution)/shard_map/ppermute | solution.py:394
  9.3 2.6 %collective-permute-start.9 = (f32[4,64,128]{2,1,0:T(8,128)S(1)}, f32[4,64,128]{2,1,0:T(8,128)S(1)}, u32[]{:S(2)}, u32[]{:S(2)}) collective-permute-start(f32[4,64,128]{2,1,0:T(8,128)S(1)} %get-tuple-element.43), channel_id=1, source_target_pairs={{0,16},{8,24},{16,0},{24,8},{1,17},{9,25},{17,1},{25,9},{2,18},{10... | collective-permute-start | bytes 393224 | tf_op jit(solution)/shard_map/ppermute | solution.py:394
  11.9 1.3 %collective-permute-start.10 = (f32[4,64,128]{2,1,0:T(8,128)S(1)}, f32[4,64,128]{2,1,0:T(8,128)S(1)}, u32[]{:S(2)}, u32[]{:S(2)}) collective-permute-start(f32[4,64,128]{2,1,0:T(8,128)S(1)} %get-tuple-element.44), channel_id=1, source_target_pairs={{0,24},{8,0},{16,8},{24,16},{1,25},{9,1},{17,9},{25,17},{2,26},{10... | collective-permute-start | bytes 393224 | tf_op jit(solution)/shard_map/ppermute | solution.py:394
  13.2 2.2 %tally.1 = f32[8,2,8,128]{3,2,1,0:T(8,128)} custom-call(f32[10,128]{1,0:T(8,128)} %bitcast.22, f32[10,128]{1,0:T(8,128)} %bitcast.23, s32[1,1280]{1,0:T(1,128)} %bitcast.25, s32[10,128]{1,0:T(8,128)} %bitcast.24), custom_call_target="tpu_custom_call" | custom-call | tf_op jit(solution)/shard_map/tally/pallas_call | solution.py:240
  15.4 0.0 copy-start.1
  15.5 0.0 copy-start.2
  15.5 3.4 %all-to-all-start = ((f32[8,2,8,128]{3,2,1,0:T(8,128)}), f32[8,2,8,128]{3,2,1,0:T(8,128)S(1)}, u32[]{:S(2)}, u32[]{:S(2)}) async-start(f32[8,2,8,128]{3,2,1,0:T(8,128)} %tally.1), calls=%async_computation | async-start | bytes 131072 | tf_op jit(solution)/shard_map/all_to_all | solution.py:402
  18.8 0.0 collective-permute-done.refs_5_
  18.9 0.0 collective-permute-done.1.refs_6_
  18.9 0.0 copy-done
  18.9 0.0 copy-done.1
  18.9 0.0 copy-done.2
  18.9 1.1 %outer.1 = (f32[4,64,128]{2,1,0:T(8,128)S(1)}, f32[4,64,128]{2,1,0:T(8,128)S(1)}, f32[4,64,128]{2,1,0:T(8,128)S(1)}, f32[4,64,128]{2,1,0:T(8,128)S(1)}) custom-call(s32[1]{0:T(128)} %bitcast.refs_0_.place, f32[64,32,128]{2,1,0:T(8,128)S(1)} %copy-done, ...), custom_call_target="tpu_custom_call", output_to_operand_aliasing={{0}: (7, {}), {1}: (8, {}), {2}: (9, {}), {3}: (10, {})} | custom-call | tf_op jit(solution)/shard_map/outer/pallas_call | solution.py:178
  20.0 0.7 %collective-permute-start.2 = (f32[4,64,128]{2,1,0:T(8,128)S(1)}, f32[4,64,128]{2,1,0:T(8,128)S(1)}, u32[]{:S(2)}, u32[]{:S(2)}) collective-permute-start(f32[4,64,128]{2,1,0:T(8,128)S(1)} %get-tuple-element.34), channel_id=1, source_target_pairs={{0,8},{8,16},{16,24},{24,0},{1,9},{9,17},{17,25},{25,1},{2,10},{10... | collective-permute-start | bytes 393224 | tf_op jit(solution)/shard_map/ppermute | solution.py:394
  20.7 0.3 collective-permute-start.3
  21.1 0.0 collective-permute-done.8.refs_1_
  21.1 2.8 %collective-permute-start.4 = (f32[4,64,128]{2,1,0:T(8,128)S(1)}, f32[4,64,128]{2,1,0:T(8,128)S(1)}, u32[]{:S(2)}, u32[]{:S(2)}) collective-permute-start(f32[4,64,128]{2,1,0:T(8,128)S(1)} %get-tuple-element.36), channel_id=1, source_target_pairs={{0,24},{8,0},{16,8},{24,16},{1,25},{9,1},{17,9},{25,17},{2,26},{10... | collective-permute-start | bytes 393224 | tf_op jit(solution)/shard_map/ppermute | solution.py:394
  23.9 0.0 all-to-all-done.tallies_ref
  23.9 0.0 collective-permute-done.9.refs_2_
  23.9 0.0 collective-permute-done.10.refs_3_
  23.9 3.3 %shard_map.74 = (f32[256,128]{1,0:T(8,128)S(1)}, f32[256,128]{1,0:T(8,128)S(1)}, f32[256,128]{1,0:T(8,128)S(1)}, f32[256,128]{1,0:T(8,128)S(1)}) custom-call(s32[1]{0:T(128)} %bitcast.refs_0_.place, f32[8,2,8,128]{3,2,1,0:T(8,128)S(1)} %all-to-all-done.tallies_ref, f32[4,64,128]{2,1,0:T(8,128)S(1)} %get-tuple-element.41.refs_0_, ...), custom_call_target="tpu_custom_call" | custom-call | tf_op jit(solution)/shard_map/pallas_call | solution.py:344
  27.2 1.3 %collective-permute-start.11 = (f32[256,128]{1,0:T(8,128)S(1)}, f32[256,128]{1,0:T(8,128)S(1)}, u32[]{:S(2)}, u32[]{:S(2)}) collective-permute-start(f32[256,128]{1,0:T(8,128)S(1)} %get-tuple-element.46), channel_id=1, source_target_pairs={{0,24},{8,0},{16,8},{24,16},{1,25},{9,1},{17,9},{25,17},{2,26},{10... | collective-permute-start | bytes 393224 | tf_op jit(solution)/shard_map/ppermute | solution.py:394
  28.5 0.9 %collective-permute-start.12 = (f32[256,128]{1,0:T(8,128)S(1)}, f32[256,128]{1,0:T(8,128)S(1)}, u32[]{:S(2)}, u32[]{:S(2)}) collective-permute-start(f32[256,128]{1,0:T(8,128)S(1)} %get-tuple-element.47), channel_id=1, source_target_pairs={{0,16},{8,24},{16,0},{24,8},{1,17},{9,25},{17,1},{25,9},{2,18},{10... | collective-permute-start | bytes 393224 | tf_op jit(solution)/shard_map/ppermute | solution.py:394
  29.4 0.0 collective-permute-done.2.refs_1_
  29.4 1.9 %collective-permute-start.13 = (f32[256,128]{1,0:T(8,128)S(1)}, f32[256,128]{1,0:T(8,128)S(1)}, u32[]{:S(2)}, u32[]{:S(2)}) collective-permute-start(f32[256,128]{1,0:T(8,128)S(1)} %get-tuple-element.48), channel_id=1, source_target_pairs={{0,8},{8,16},{16,24},{24,0},{1,9},{9,17},{17,25},{25,1},{2,10},{10... | collective-permute-start | bytes 393224 | tf_op jit(solution)/shard_map/ppermute | solution.py:394
  31.3 2.1 %collective-permute-done.3.refs_2_ = f32[4,64,128]{2,1,0:T(8,128)S(1)} collective-permute-done((f32[4,64,128]{2,1,0:T(8,128)S(1)}, f32[4,64,128]{2,1,0:T(8,128)S(1)}, u32[]{:S(2)}, u32[]{:S(2)}) %collective-permute-start.3) | collective-permute-done | bytes 131104 | tf_op jit(solution)/shard_map/ppermute | solution.py:394
  33.4 0.0 collective-permute-done.4.refs_3_
  33.4 3.3 %shard_map.73 = (f32[256,128]{1,0:T(8,128)S(1)}, f32[256,128]{1,0:T(8,128)S(1)}, f32[256,128]{1,0:T(8,128)S(1)}, f32[256,128]{1,0:T(8,128)S(1)}) custom-call(s32[1]{0:T(128)} %bitcast.refs_0_.place, f32[8,2,8,128]{3,2,1,0:T(8,128)S(1)} %all-to-all-done.tallies_ref, f32[4,64,128]{2,1,0:T(8,128)S(1)} %get-tuple-element.33.refs_0_, ...), custom_call_target="tpu_custom_call" | custom-call | tf_op jit(solution)/shard_map/pallas_call | solution.py:344
  36.8 8.7 %collective-permute-start.5 = (f32[256,128]{1,0:T(8,128)S(1)}, f32[256,128]{1,0:T(8,128)S(1)}, u32[]{:S(2)}, u32[]{:S(2)}) collective-permute-start(f32[256,128]{1,0:T(8,128)S(1)} %get-tuple-element.38), channel_id=1, source_target_pairs={{0,24},{8,0},{16,8},{24,16},{1,25},{9,1},{17,9},{25,17},{2,26},{10... | collective-permute-start | bytes 393224 | tf_op jit(solution)/shard_map/ppermute | solution.py:394
  45.5 0.0 collective-permute-start.6
  45.5 0.0 collective-permute-done.11
  45.5 0.6 %collective-permute-start.7 = (f32[256,128]{1,0:T(8,128)S(1)}, f32[256,128]{1,0:T(8,128)S(1)}, u32[]{:S(2)}, u32[]{:S(2)}) collective-permute-start(f32[256,128]{1,0:T(8,128)S(1)} %get-tuple-element.40), channel_id=1, source_target_pairs={{0,8},{8,16},{16,24},{24,0},{1,9},{9,17},{17,25},{25,1},{2,10},{10... | collective-permute-start | bytes 393224 | tf_op jit(solution)/shard_map/ppermute | solution.py:394
  46.1 2.4 %collective-permute-done.12 = f32[256,128]{1,0:T(8,128)S(1)} collective-permute-done((f32[256,128]{1,0:T(8,128)S(1)}, f32[256,128]{1,0:T(8,128)S(1)}, u32[]{:S(2)}, u32[]{:S(2)}) %collective-permute-start.12) | collective-permute-done | bytes 131104 | tf_op jit(solution)/shard_map/ppermute | solution.py:394
  48.6 0.0 collective-permute-done.13
  48.6 0.8 %shard_map.75.refs_4_ = f32[64,8,4,128]{3,2,1,0:T(4,128)} custom-call(s32[1]{0:T(128)} %bitcast.refs_0_.place, f32[64,4,128]{2,1,0:T(4,128)S(1)} %bitcast.14, f32[64,4,128]{2,1,0:T(4,128)S(1)} %bitcast.15, f32[64,4,128]{2,1,0:T(4,128)S(1)} %bitcast.16, f32[64,4,128]{2,1,0:T(4,128)S(1)} %bitcast.18), custom_call_target="tpu_custom_call" | custom-call | tf_op jit(solution)/shard_map/pallas_call | solution.py:371
  49.4 0.0 collective-permute-done.5
  49.4 8.7 %collective-permute-done.6 = f32[256,128]{1,0:T(8,128)S(1)} collective-permute-done((f32[256,128]{1,0:T(8,128)S(1)}, f32[256,128]{1,0:T(8,128)S(1)}, u32[]{:S(2)}, u32[]{:S(2)}) %collective-permute-start.6) | collective-permute-done | bytes 131104 | tf_op jit(solution)/shard_map/ppermute | solution.py:394
  58.2 0.0 collective-permute-done.7
  58.2 0.8 %shard_map.76 = f32[64,8,4,128]{3,2,1,0:T(4,128)} custom-call(s32[1]{0:T(128)} %bitcast.refs_0_.place, f32[64,4,128]{2,1,0:T(4,128)S(1)} %bitcast.17, f32[64,4,128]{2,1,0:T(4,128)S(1)} %bitcast.19, f32[64,4,128]{2,1,0:T(4,128)S(1)} %bitcast.20, f32[64,4,128]{2,1,0:T(4,128)S(1)} %bitcast.21, ...), custom_call_target="tpu_custom_call", output_to_operand_aliasing={{}: (5, {})} | custom-call | tf_op jit(solution)/shard_map/pallas_call | solution.py:371
Async XLA Ops:
  0.0 18.9 %copy-start = (f32[64,32,128]{2,1,0:T(8,128)S(1)}, f32[64,32,128]{2,1,0:T(8,128)}, u32[]{:S(2)}) copy-start(f32[64,32,128]{2,1,0:T(8,128)} %refs_2_.3) | copy-start | bytes 3145732
  3.5 15.3 %collective-permute-start = (f32[4,72,128]{2,1,0:T(8,128)S(1)}, f32[4,72,128]{2,1,0:T(8,128)S(1)}, u32[]{:S(2)}, u32[]{:S(2)}) collective-permute-start(f32[4,72,128]{2,1,0:T(8,128)S(1)} %get-tuple-element.27), channel_id=1, source_target_pairs={{0,1},{1,2},{2,3},{3,4},{4,5},{5,6},{6,7},{7,0},{8,9},{9,10},{10,1... | collective-permute-start | bytes 442376 | tf_op jit(solution)/shard_map/ppermute | solution.py:399
  4.1 14.8 %collective-permute-start.1 = (f32[4,72,128]{2,1,0:T(8,128)S(1)}, f32[4,72,128]{2,1,0:T(8,128)S(1)}, u32[]{:S(2)}, u32[]{:S(2)}) collective-permute-start(f32[4,72,128]{2,1,0:T(8,128)S(1)} %get-tuple-element.28), channel_id=1, source_target_pairs={{1,0},{2,1},{3,2},{4,3},{5,4},{6,5},{7,6},{0,7},{9,8},{10,9},{11,1... | collective-permute-start | bytes 442376 | tf_op jit(solution)/shard_map/ppermute | solution.py:400
  7.0 14.0 %collective-permute-start.8 = (f32[4,64,128]{2,1,0:T(8,128)S(1)}, f32[4,64,128]{2,1,0:T(8,128)S(1)}, u32[]{:S(2)}, u32[]{:S(2)}) collective-permute-start(f32[4,64,128]{2,1,0:T(8,128)S(1)} %get-tuple-element.42), channel_id=1, source_target_pairs={{0,8},{8,16},{16,24},{24,0},{1,9},{9,17},{17,25},{25,1},{2,10},{10... | collective-permute-start | bytes 393224 | tf_op jit(solution)/shard_map/ppermute | solution.py:394
  9.3 14.6 %collective-permute-start.9 = (f32[4,64,128]{2,1,0:T(8,128)S(1)}, f32[4,64,128]{2,1,0:T(8,128)S(1)}, u32[]{:S(2)}, u32[]{:S(2)}) collective-permute-start(f32[4,64,128]{2,1,0:T(8,128)S(1)} %get-tuple-element.43), channel_id=1, source_target_pairs={{0,16},{8,24},{16,0},{24,8},{1,17},{9,25},{17,1},{25,9},{2,18},{10... | collective-permute-start | bytes 393224 | tf_op jit(solution)/shard_map/ppermute | solution.py:394
  11.9 12.0 %collective-permute-start.10 = (f32[4,64,128]{2,1,0:T(8,128)S(1)}, f32[4,64,128]{2,1,0:T(8,128)S(1)}, u32[]{:S(2)}, u32[]{:S(2)}) collective-permute-start(f32[4,64,128]{2,1,0:T(8,128)S(1)} %get-tuple-element.44), channel_id=1, source_target_pairs={{0,24},{8,0},{16,8},{24,16},{1,25},{9,1},{17,9},{25,17},{2,26},{10... | collective-permute-start | bytes 393224 | tf_op jit(solution)/shard_map/ppermute | solution.py:394
  15.4 3.4 %copy-start.1 = (f32[2,32,128]{2,1,0:T(8,128)S(1)}, f32[2,32,128]{2,1,0:T(8,128)}, u32[]{:S(2)}) copy-start(f32[2,32,128]{2,1,0:T(8,128)} %refs_4_.1) | copy-start | bytes 98308
  15.5 3.4 %copy-start.2 = (f32[32,128]{1,0:T(8,128)S(1)}, f32[32,128]{1,0:T(8,128)}, u32[]{:S(2)}) copy-start(f32[32,128]{1,0:T(8,128)} %refs_3_.3) | copy-start | bytes 49156
  15.5 8.4 %all-to-all-start = ((f32[8,2,8,128]{3,2,1,0:T(8,128)}), f32[8,2,8,128]{3,2,1,0:T(8,128)S(1)}, u32[]{:S(2)}, u32[]{:S(2)}) async-start(f32[8,2,8,128]{3,2,1,0:T(8,128)} %tally.1), calls=%async_computation | async-start | bytes 131072 | tf_op jit(solution)/shard_map/all_to_all | solution.py:402
  20.0 9.4 %collective-permute-start.2 = (f32[4,64,128]{2,1,0:T(8,128)S(1)}, f32[4,64,128]{2,1,0:T(8,128)S(1)}, u32[]{:S(2)}, u32[]{:S(2)}) collective-permute-start(f32[4,64,128]{2,1,0:T(8,128)S(1)} %get-tuple-element.34), channel_id=1, source_target_pairs={{0,8},{8,16},{16,24},{24,0},{1,9},{9,17},{17,25},{25,1},{2,10},{10... | collective-permute-start | bytes 393224 | tf_op jit(solution)/shard_map/ppermute | solution.py:394
  20.7 12.7 %collective-permute-start.3 = (f32[4,64,128]{2,1,0:T(8,128)S(1)}, f32[4,64,128]{2,1,0:T(8,128)S(1)}, u32[]{:S(2)}, u32[]{:S(2)}) collective-permute-start(f32[4,64,128]{2,1,0:T(8,128)S(1)} %get-tuple-element.35), channel_id=1, source_target_pairs={{0,16},{8,24},{16,0},{24,8},{1,17},{9,25},{17,1},{25,9},{2,18},{10... | collective-permute-start | bytes 393224 | tf_op jit(solution)/shard_map/ppermute | solution.py:394
  21.1 12.4 %collective-permute-start.4 = (f32[4,64,128]{2,1,0:T(8,128)S(1)}, f32[4,64,128]{2,1,0:T(8,128)S(1)}, u32[]{:S(2)}, u32[]{:S(2)}) collective-permute-start(f32[4,64,128]{2,1,0:T(8,128)S(1)} %get-tuple-element.36), channel_id=1, source_target_pairs={{0,24},{8,0},{16,8},{24,16},{1,25},{9,1},{17,9},{25,17},{2,26},{10... | collective-permute-start | bytes 393224 | tf_op jit(solution)/shard_map/ppermute | solution.py:394
  27.2 18.3 %collective-permute-start.11 = (f32[256,128]{1,0:T(8,128)S(1)}, f32[256,128]{1,0:T(8,128)S(1)}, u32[]{:S(2)}, u32[]{:S(2)}) collective-permute-start(f32[256,128]{1,0:T(8,128)S(1)} %get-tuple-element.46), channel_id=1, source_target_pairs={{0,24},{8,0},{16,8},{24,16},{1,25},{9,1},{17,9},{25,17},{2,26},{10... | collective-permute-start | bytes 393224 | tf_op jit(solution)/shard_map/ppermute | solution.py:394
  28.5 20.1 %collective-permute-start.12 = (f32[256,128]{1,0:T(8,128)S(1)}, f32[256,128]{1,0:T(8,128)S(1)}, u32[]{:S(2)}, u32[]{:S(2)}) collective-permute-start(f32[256,128]{1,0:T(8,128)S(1)} %get-tuple-element.47), channel_id=1, source_target_pairs={{0,16},{8,24},{16,0},{24,8},{1,17},{9,25},{17,1},{25,9},{2,18},{10... | collective-permute-start | bytes 393224 | tf_op jit(solution)/shard_map/ppermute | solution.py:394
  29.4 19.2 %collective-permute-start.13 = (f32[256,128]{1,0:T(8,128)S(1)}, f32[256,128]{1,0:T(8,128)S(1)}, u32[]{:S(2)}, u32[]{:S(2)}) collective-permute-start(f32[256,128]{1,0:T(8,128)S(1)} %get-tuple-element.48), channel_id=1, source_target_pairs={{0,8},{8,16},{16,24},{24,0},{1,9},{9,17},{17,25},{25,1},{2,10},{10... | collective-permute-start | bytes 393224 | tf_op jit(solution)/shard_map/ppermute | solution.py:394
  36.8 12.7 %collective-permute-start.5 = (f32[256,128]{1,0:T(8,128)S(1)}, f32[256,128]{1,0:T(8,128)S(1)}, u32[]{:S(2)}, u32[]{:S(2)}) collective-permute-start(f32[256,128]{1,0:T(8,128)S(1)} %get-tuple-element.38), channel_id=1, source_target_pairs={{0,24},{8,0},{16,8},{24,16},{1,25},{9,1},{17,9},{25,17},{2,26},{10... | collective-permute-start | bytes 393224 | tf_op jit(solution)/shard_map/ppermute | solution.py:394
  45.5 12.7 %collective-permute-start.6 = (f32[256,128]{1,0:T(8,128)S(1)}, f32[256,128]{1,0:T(8,128)S(1)}, u32[]{:S(2)}, u32[]{:S(2)}) collective-permute-start(f32[256,128]{1,0:T(8,128)S(1)} %get-tuple-element.39), channel_id=1, source_target_pairs={{0,16},{8,24},{16,0},{24,8},{1,17},{9,25},{17,1},{25,9},{2,18},{10... | collective-permute-start | bytes 393224 | tf_op jit(solution)/shard_map/ppermute | solution.py:394
  45.5 12.7 %collective-permute-start.7 = (f32[256,128]{1,0:T(8,128)S(1)}, f32[256,128]{1,0:T(8,128)S(1)}, u32[]{:S(2)}, u32[]{:S(2)}) collective-permute-start(f32[256,128]{1,0:T(8,128)S(1)} %get-tuple-element.40), channel_id=1, source_target_pairs={{0,8},{8,16},{16,24},{24,0},{1,9},{9,17},{17,25},{25,1},{2,10},{10... | collective-permute-start | bytes 393224 | tf_op jit(solution)/shard_map/ppermute | solution.py:394
where the time goes:
time: 59.3 us; the launch traced here: 59 us
  starting transfers between devices  30.4 us (51%)
  Pallas kernels  15.1 us (25%)
  waiting for transfers between devices  13.3 us (22%)
    ppermute x12, starting transfers between devices, send(): moved.append(lax.ppermute(parts[shift], 'mem', ways))  23.6 us
    ppermute x12, waiting for transfers between devices, send(): moved.append(lax.ppermute(parts[shift], 'mem', ways))  13.3 us
    pallas_call x2, Pallas kernels, analyse(): pl.pallas_call(functools.partial(analyse_kernel, chunk, n_mem), in_specs=...  6.63 us
    pallas_call x1, Pallas kernels, inner(): pl.pallas_call(functools.partial(inner_kernel, n_mem), in_specs=[SMEM] +...  3.53 us
    all_to_all x1, starting transfers between devices, shards(): lax.all_to_all(counts, 'slab', split_axis=0, concat_axis=0, tiled=True)  3.36 us
    ppermute x1, starting transfers between devices, shards(): below = lax.ppermute(head, 'slab', down)  2.93 us
    pallas_call x1, Pallas kernels, tally(): pl.pallas_call(tally_kernel, in_specs=[HBM] * 4, out_specs=VMEM, out_shap...  2.21 us
    pallas_call x2, Pallas kernels, settle(): pl.pallas_call(functools.partial(settle_kernel, chunk, n_mem), in_specs=[...  1.64 us
  transfers between devices with their start and end apart: 15, of which 3 were waited for; matrix products, arithmetic and copies ran while one was open for 0% of the time, Pallas kernels for 18%

commit v1 on v0

--- a/solution.py
+++ b/solution.py
@@ -63,28 +63,60 @@
     return source
 
 
+def tally(value_ref, weight_ref, slab_ref, cell_ref, out_ref):
+    n_slab, _, _, width = out_ref.shape
+    blocks, lanes = value_ref.shape
+    bins = n_slab * SUB
+    bin_id = lax.broadcasted_iota(jnp.int32, (bins, lanes), 0)
+    column_id = lax.broadcasted_iota(jnp.int32, (width, lanes), 0)
+    totals = jnp.zeros((2 * bins, width), F32)
+    for b in range(blocks):
+        cell = cell_ref[b : b + 1, :]
+        weight = weight_ref[b : b + 1, :]
+        product = weight * value_ref[b : b + 1, :]
+        named = slab_ref[:, pl.ds(b * lanes, lanes)] * SUB + cell // width
+        here = bin_id == named
+        column = jnp.where(column_id == cell % width, 1.0, 0.0).astype(BF16)
+        rest = jnp.concatenate(
+            [jnp.where(here, weight, 0.0), jnp.where(here, product, 0.0)], axis=0
+        )
+        for _ in range(3):
+            piece = rest.astype(BF16)
+            rest = rest - piece.astype(F32)
+            totals = totals + lax.dot_general(
+                piece, column, (((1,), (1,)), ((), ())), preferred_element_type=F32
+            )
+    for k in range(2 * n_slab):
+        out_ref[k % n_slab, k // n_slab] = totals[k * SUB : (k + 1) * SUB]
+
+
 def inner_kernel(n_mem, *refs):
-    place, ens_hbm, diffuse_hbm, drift_hbm = refs[:4]
-    edges, early, late = refs[4:6], refs[6 : 6 + n_mem], refs[6 + n_mem : 6 + 2 * n_mem]
-    field, table, ping, pong, ens_ref, diffuse_ref, drift_ref, sems = refs[6 + 2 * n_mem :]
+    place, ens_hbm, rest = refs[0], refs[1], refs[2:8]
+    refs = refs[8:]
+    counts, edges = refs[0], refs[1:3]
+    early, late = refs[3 : 3 + n_mem], refs[3 + n_mem : 3 + 2 * n_mem]
+    field, table, ping, pong, ens_ref, sems = refs[3 + 2 * n_mem : 9 + 2 * n_mem]
+    small = refs[9 + 2 * n_mem :]
+    diffuse_ref, drift_ref = small[:2]
     rows, width = diffuse_ref.shape
     members = ens_hbm.shape[0]
 
     copies = [
-        pltpu.make_async_copy(diffuse_hbm, diffuse_ref, sems.at[n_mem]),
-        pltpu.make_async_copy(drift_hbm, drift_ref, sems.at[n_mem + 1]),
+        pltpu.make_async_copy(source, target, sems.at[n_mem + k])
+        for k, (source, target) in enumerate(zip(rest, small))
     ]
-    for g in range(n_mem):
-        copies.append(
-            pltpu.make_async_copy(ens_hbm.at[:, pl.ds(g * SUB, SUB)], ens_ref.at[g], sems.at[g])
-        )
+    copies += [
+        pltpu.make_async_copy(ens_hbm.at[:, pl.ds(g * SUB, SUB)], ens_ref.at[g], sems.at[g])
+        for g in range(n_mem)
+    ]
     for copy in copies:
         copy.start()
-    copies[0].wait()
-    copies[1].wait()
+    for copy in copies[: len(rest)]:
+        copy.wait()
     put_table(table, 0, diffuse_ref[...], drift_ref[0], drift_ref[1])
+    tally(*small[2:], counts)
     for g in range(n_mem):
-        copies[2 + g].wait()
+        copies[len(rest) + g].wait()
         group = ens_ref.at[g].reshape(members * SUB, width)
         for r in range(SUB):
             field[g * SUB + r] = group[pl.ds(r, members, stride=SUB), :]
@@ -106,15 +138,17 @@
             late[shift][r] = done[bottom + r]
 
 
-def inner(n_mem, place, ens, diffusivity, velocity):
+def inner(n_mem, n_slab, place, ens, diffusivity, velocity, value, weight, slab, cell):
     rows, width = diffusivity.shape
     members = ens.shape[0]
+    value, weight, cell = (a.reshape(-1, width) for a in (value, weight, cell))
+    small = [diffusivity, velocity, value, weight, slab.reshape(1, -1), cell]
     part = pltpu.VMEM((HALF, members, width), F32)
     edge = pltpu.VMEM((STEPS, members + SUB, width), F32)
-    shapes = [edge] * 2 + [part] * (2 * n_mem)
+    shapes = [pltpu.VMEM((n_slab, 2, SUB, width), F32)] + [edge] * 2 + [part] * (2 * n_mem)
     outs = pl.pallas_call(
         functools.partial(inner_kernel, n_mem),
-        in_specs=[SMEM] + [HBM] * 3,
+        in_specs=[SMEM] + [HBM] * (1 + len(small)),
         out_specs=[VMEM] * len(shapes),
         out_shape=shapes,
         scratch_shapes=[
@@ -123,14 +157,13 @@
             pltpu.VMEM((rows, members, width), F32),
             pltpu.VMEM((rows, members, width), F32),
             pltpu.VMEM((n_mem, members, SUB, width), F32),
-            pltpu.VMEM(diffusivity.shape, F32),
-            pltpu.VMEM(velocity.shape, F32),
-            pltpu.SemaphoreType.DMA((n_mem + 2,)),
-        ],
+            pltpu.SemaphoreType.DMA((n_mem + len(small),)),
+        ]
+        + [pltpu.VMEM(a.shape, a.dtype) for a in small],
         compiler_params=PARAMS,
         name="inner",
-    )(place, *far([ens, diffusivity, velocity]))
-    return outs[:2], outs[2 : 2 + n_mem], outs[2 + n_mem :]
+    )(place, *far([ens, *small]))
+    return outs[0], outs[1:3], outs[3 : 3 + n_mem], outs[3 + n_mem :]
 
 
 def outer_kernel(n_mem, *refs):
@@ -199,56 +232,6 @@
     )(place, ens, ens, diffusivity, velocity, *near(halos), *late)
 
 
-def tally_kernel(*refs):
-    out_ref, sems, value_ref, weight_ref, slab_ref, cell_ref = refs[4:]
-    copies = [pltpu.make_async_copy(refs[k], refs[6 + k], sems.at[k]) for k in range(4)]
-    for copy in copies:
-        copy.start()
-    for copy in copies:
-        copy.wait()
-    lanes = out_ref.shape[-1]
-    blocks = value_ref.shape[0]
-    n_slab = out_ref.shape[0]
-    width = out_ref.shape[-1]
-    bins = n_slab * SUB
-    bin_id = lax.broadcasted_iota(jnp.int32, (bins, lanes), 0)
-    column_id = lax.broadcasted_iota(jnp.int32, (width, lanes), 0)
-    totals = jnp.zeros((2 * bins, width), F32)
-    for b in range(blocks):
-        cell = cell_ref[b : b + 1, :]
-        weight = weight_ref[b : b + 1, :]
-        product = weight * value_ref[b : b + 1, :]
-        named = slab_ref[:, pl.ds(b * lanes, lanes)] * SUB + cell // width
-        here = bin_id == named
-        column = jnp.where(column_id == cell % width, 1.0, 0.0).astype(BF16)
-        rest = jnp.concatenate(
-            [jnp.where(here, weight, 0.0), jnp.where(here, product, 0.0)], axis=0
-        )
-        for _ in range(3):
-            piece = rest.astype(BF16)
-            rest = rest - piece.astype(F32)
-            totals = totals + lax.dot_general(
-                piece, column, (((1,), (1,)), ((), ())), preferred_element_type=F32
-            )
-    for k in range(2 * n_slab):
-        out_ref[k % n_slab, k // n_slab] = totals[k * SUB : (k + 1) * SUB]
-
-
-def tally(value, weight, slab, cell, n_slab, width):
-    value, weight, cell = (a.reshape(-1, width) for a in (value, weight, cell))
-    arrays = [value, weight, slab.reshape(1, -1), cell]
-    return pl.pallas_call(
-        tally_kernel,
-        in_specs=[HBM] * 4,
-        out_specs=VMEM,
-        out_shape=pltpu.VMEM((n_slab, 2, SUB, width), F32),
-        scratch_shapes=[pltpu.SemaphoreType.DMA((4,))]
-        + [pltpu.VMEM(a.shape, a.dtype) for a in arrays],
-        compiler_params=PARAMS,
-        name="tally",
-    )(*far(arrays))
-
-
 def halves(a):
     high = a.astype(BF16)
     return high, (a - high.astype(F32)).astype(BF16)
@@ -394,11 +377,21 @@
             moved.append(lax.ppermute(parts[shift], "mem", ways))
         return moved
 
-    (head, tail), early, late = inner(n_mem, place, ensemble, diffusivity, velocity)
+    counts, (head, tail), early, late = inner(
+        n_mem,
+        n_slab,
+        place,
+        ensemble,
+        diffusivity,
+        velocity,
+        obs_value,
+        obs_weight,
+        obs_slab,
+        obs_cell,
+    )
     early = send(early, 1)
     above = lax.ppermute(tail, "slab", up)
     below = lax.ppermute(head, "slab", down)
-    counts = tally(obs_value, obs_weight, obs_slab, obs_cell, n_slab, width)
     counts = lax.all_to_all(counts, "slab", split_axis=0, concat_axis=0, tiled=True)
     late = outer(n_mem, place, ensemble, diffusivity, velocity, (above, below), late)
     late = send(late, 1)

time: 59.3 us -> 57.9 us (0.976)
  starting transfers between devices: 30.4 us -> 35 us
  waiting for transfers between devices: 13.3 us -> 9.02 us
  Pallas kernels: 15.1 us -> 13.5 us
    ppermute x12, starting transfers between devices: 23.6 us -> 28 us  [send(): moved.append(lax.ppermute(parts[shift], 'mem', ways))]
    ppermute x12, waiting for transfers between devices: 13.3 us -> 9.01 us  [send(): moved.append(lax.ppermute(parts[shift], 'mem', ways))]
    pallas_call x1 -> x0, Pallas kernels: 2.21 us -> none  [tally(): pl.pallas_call(tally_kernel, in_specs=[HBM] * 4, out_specs=VMEM, out_shap...]
  transfers between devices with their start and end apart: 15 -> 15, of which waited for: 3 -> 3; matrix products, arithmetic and copies ran while one was open for 0% -> 0% of each run, Pallas kernels for 18% -> 15%
where the time goes in v1:
time: 57.9 us; the launch traced here: 57.6 us
  starting transfers between devices  35 us (60%)
  Pallas kernels  13.5 us (23%)
  waiting for transfers between devices  9.02 us (16%)
    ppermute x12, starting transfers between devices, send(): moved.append(lax.ppermute(parts[shift], 'mem', ways))  28 us
    ppermute x12, waiting for transfers between devices, send(): moved.append(lax.ppermute(parts[shift], 'mem', ways))  9.01 us
    pallas_call x2, Pallas kernels, analyse(): pl.pallas_call(functools.partial(analyse_kernel, chunk, n_mem), in_specs=...  6.61 us
    pallas_call x1, Pallas kernels, inner(): pl.pallas_call(functools.partial(inner_kernel, n_mem), in_specs=[SMEM] +...  4.12 us
    all_to_all x1, starting transfers between devices, shards(): lax.all_to_all(counts, 'slab', split_axis=0, concat_axis=0, tiled=True)  3.48 us
    ppermute x1, starting transfers between devices, shards(): below = lax.ppermute(head, 'slab', down)  2.94 us
    pallas_call x2, Pallas kernels, settle(): pl.pallas_call(functools.partial(settle_kernel, chunk, n_mem), in_specs=[...  1.64 us
  transfers between devices with their start and end apart: 15, of which 3 were waited for; matrix products, arithmetic and copies ran while one was open for 0% of the time, Pallas kernels for 15%

profile of v1, /device:TPU:0, one launch (start us, length us, event | category | flops | bytes accessed | tf_op | source)
XLA Modules:
  0.0 57.6 jit_solution(2868946883278981649)
XLA Ops:
  0.0 0.0 copy-start
  0.0 4.1 %inner.1 = (f32[8,2,8,128]{3,2,1,0:T(8,128)}, f32[4,72,128]{2,1,0:T(8,128)S(1)}, f32[4,72,128]{2,1,0:T(8,128)S(1)}, f32[4,64,128]{2,1,0:T(8,128)S(1)}, f32[4,64,...) custom-call(s32[1]{0:T(128)} %bitcast.refs_0_.place, ...), custom_call_target="tpu_custom_call" | custom-call | tf_op jit(solution)/shard_map/inner/pallas_call | solution.py:149
  4.1 0.5 collective-permute-start
  4.7 2.9 %collective-permute-start.1 = (f32[4,72,128]{2,1,0:T(8,128)S(1)}, f32[4,72,128]{2,1,0:T(8,128)S(1)}, u32[]{:S(2)}, u32[]{:S(2)}) collective-permute-start(f32[4,72,128]{2,1,0:T(8,128)S(1)} %get-tuple-element.30), channel_id=1, source_target_pairs={{1,0},{2,1},{3,2},{4,3},{5,4},{6,5},{7,6},{0,7},{9,8},{10,9},{11,1... | collective-permute-start | bytes 442376 | tf_op jit(solution)/shard_map/ppermute | solution.py:394
  7.6 2.3 %collective-permute-start.8 = (f32[4,64,128]{2,1,0:T(8,128)S(1)}, f32[4,64,128]{2,1,0:T(8,128)S(1)}, u32[]{:S(2)}, u32[]{:S(2)}) collective-permute-start(f32[4,64,128]{2,1,0:T(8,128)S(1)} %get-tuple-element.44), channel_id=1, source_target_pairs={{0,8},{8,16},{16,24},{24,0},{1,9},{9,17},{17,25},{25,1},{2,10},{10... | collective-permute-start | bytes 393224 | tf_op jit(solution)/shard_map/ppermute | solution.py:377
  9.9 2.6 %collective-permute-start.9 = (f32[4,64,128]{2,1,0:T(8,128)S(1)}, f32[4,64,128]{2,1,0:T(8,128)S(1)}, u32[]{:S(2)}, u32[]{:S(2)}) collective-permute-start(f32[4,64,128]{2,1,0:T(8,128)S(1)} %get-tuple-element.45), channel_id=1, source_target_pairs={{0,16},{8,24},{16,0},{24,8},{1,17},{9,25},{17,1},{25,9},{2,18},{10... | collective-permute-start | bytes 393224 | tf_op jit(solution)/shard_map/ppermute | solution.py:377
  12.5 1.3 %collective-permute-start.10 = (f32[4,64,128]{2,1,0:T(8,128)S(1)}, f32[4,64,128]{2,1,0:T(8,128)S(1)}, u32[]{:S(2)}, u32[]{:S(2)}) collective-permute-start(f32[4,64,128]{2,1,0:T(8,128)S(1)} %get-tuple-element.46), channel_id=1, source_target_pairs={{0,24},{8,0},{16,8},{24,16},{1,25},{9,1},{17,9},{25,17},{2,26},{10... | collective-permute-start | bytes 393224 | tf_op jit(solution)/shard_map/ppermute | solution.py:377
  13.8 0.0 copy-start.1
  13.8 0.0 copy-start.2
  13.8 3.5 %all-to-all-start = ((f32[8,2,8,128]{3,2,1,0:T(8,128)}), f32[8,2,8,128]{3,2,1,0:T(8,128)S(1)}, u32[]{:S(2)}, u32[]{:S(2)}) async-start(f32[8,2,8,128]{3,2,1,0:T(8,128)} %get-tuple-element.28), calls=%async_computation | async-start | bytes 131072 | tf_op jit(solution)/shard_map/all_to_all | solution.py:395
  17.3 0.0 collective-permute-done.refs_5_
  17.3 0.0 collective-permute-done.1.refs_6_
  17.3 0.0 copy-done
  17.3 0.0 copy-done.1
  17.4 0.0 copy-done.2
  17.4 1.1 %outer.1 = (f32[4,64,128]{2,1,0:T(8,128)S(1)}, f32[4,64,128]{2,1,0:T(8,128)S(1)}, f32[4,64,128]{2,1,0:T(8,128)S(1)}, f32[4,64,128]{2,1,0:T(8,128)S(1)}) custom-call(s32[1]{0:T(128)} %bitcast.refs_0_.place, f32[64,32,128]{2,1,0:T(8,128)S(1)} %copy-done, ...), custom_call_target="tpu_custom_call", output_to_operand_aliasing={{0}: (7, {}), {1}: (8, {}), {2}: (9, {}), {3}: (10, {})} | custom-call | tf_op jit(solution)/shard_map/outer/pallas_call | solution.py:211
  18.5 0.7 %collective-permute-start.2 = (f32[4,64,128]{2,1,0:T(8,128)S(1)}, f32[4,64,128]{2,1,0:T(8,128)S(1)}, u32[]{:S(2)}, u32[]{:S(2)}) collective-permute-start(f32[4,64,128]{2,1,0:T(8,128)S(1)} %get-tuple-element.36), channel_id=1, source_target_pairs={{0,8},{8,16},{16,24},{24,0},{1,9},{9,17},{17,25},{25,1},{2,10},{10... | collective-permute-start | bytes 393224 | tf_op jit(solution)/shard_map/ppermute | solution.py:377
  19.2 0.3 collective-permute-start.3
  19.5 0.0 collective-permute-done.8.refs_1_
  19.5 2.8 %collective-permute-start.4 = (f32[4,64,128]{2,1,0:T(8,128)S(1)}, f32[4,64,128]{2,1,0:T(8,128)S(1)}, u32[]{:S(2)}, u32[]{:S(2)}) collective-permute-start(f32[4,64,128]{2,1,0:T(8,128)S(1)} %get-tuple-element.38), channel_id=1, source_target_pairs={{0,24},{8,0},{16,8},{24,16},{1,25},{9,1},{17,9},{25,17},{2,26},{10... | collective-permute-start | bytes 393224 | tf_op jit(solution)/shard_map/ppermute | solution.py:377
  22.3 0.0 all-to-all-done.tallies_ref
  22.4 0.0 collective-permute-done.9.refs_2_
  22.4 0.0 collective-permute-done.10.refs_3_
  22.4 3.3 %shard_map.74 = (f32[256,128]{1,0:T(8,128)S(1)}, f32[256,128]{1,0:T(8,128)S(1)}, f32[256,128]{1,0:T(8,128)S(1)}, f32[256,128]{1,0:T(8,128)S(1)}) custom-call(s32[1]{0:T(128)} %bitcast.refs_0_.place, f32[8,2,8,128]{3,2,1,0:T(8,128)S(1)} %all-to-all-done.tallies_ref, f32[4,64,128]{2,1,0:T(8,128)S(1)} %get-tuple-element.43.refs_0_, ...), custom_call_target="tpu_custom_call" | custom-call | tf_op jit(solution)/shard_map/pallas_call | solution.py:327
  25.7 3.8 %collective-permute-start.11 = (f32[256,128]{1,0:T(8,128)S(1)}, f32[256,128]{1,0:T(8,128)S(1)}, u32[]{:S(2)}, u32[]{:S(2)}) collective-permute-start(f32[256,128]{1,0:T(8,128)S(1)} %get-tuple-element.48), channel_id=1, source_target_pairs={{0,24},{8,0},{16,8},{24,16},{1,25},{9,1},{17,9},{25,17},{2,26},{10... | collective-permute-start | bytes 393224 | tf_op jit(solution)/shard_map/ppermute | solution.py:377
  29.5 0.0 collective-permute-start.12
  29.5 0.0 collective-permute-done.2.refs_1_
  29.5 7.6 %collective-permute-start.13 = (f32[256,128]{1,0:T(8,128)S(1)}, f32[256,128]{1,0:T(8,128)S(1)}, u32[]{:S(2)}, u32[]{:S(2)}) collective-permute-start(f32[256,128]{1,0:T(8,128)S(1)} %get-tuple-element.50), channel_id=1, source_target_pairs={{0,8},{8,16},{16,24},{24,0},{1,9},{9,17},{17,25},{25,1},{2,10},{10... | collective-permute-start | bytes 393224 | tf_op jit(solution)/shard_map/ppermute | solution.py:377
  37.1 0.0 collective-permute-done.3.refs_2_
  37.1 0.0 collective-permute-done.4.refs_3_
  37.1 3.3 %shard_map.73 = (f32[256,128]{1,0:T(8,128)S(1)}, f32[256,128]{1,0:T(8,128)S(1)}, f32[256,128]{1,0:T(8,128)S(1)}, f32[256,128]{1,0:T(8,128)S(1)}) custom-call(s32[1]{0:T(128)} %bitcast.refs_0_.place, f32[8,2,8,128]{3,2,1,0:T(8,128)S(1)} %all-to-all-done.tallies_ref, f32[4,64,128]{2,1,0:T(8,128)S(1)} %get-tuple-element.35.refs_0_, ...), custom_call_target="tpu_custom_call" | custom-call | tf_op jit(solution)/shard_map/pallas_call | solution.py:327
  40.4 5.9 %collective-permute-start.5 = (f32[256,128]{1,0:T(8,128)S(1)}, f32[256,128]{1,0:T(8,128)S(1)}, u32[]{:S(2)}, u32[]{:S(2)}) collective-permute-start(f32[256,128]{1,0:T(8,128)S(1)} %get-tuple-element.40), channel_id=1, source_target_pairs={{0,24},{8,0},{16,8},{24,16},{1,25},{9,1},{17,9},{25,17},{2,26},{10... | collective-permute-start | bytes 393224 | tf_op jit(solution)/shard_map/ppermute | solution.py:377
  46.3 0.0 collective-permute-start.6
  46.3 0.0 collective-permute-done.11
  46.3 0.6 %collective-permute-start.7 = (f32[256,128]{1,0:T(8,128)S(1)}, f32[256,128]{1,0:T(8,128)S(1)}, u32[]{:S(2)}, u32[]{:S(2)}) collective-permute-start(f32[256,128]{1,0:T(8,128)S(1)} %get-tuple-element.42), channel_id=1, source_target_pairs={{0,8},{8,16},{16,24},{24,0},{1,9},{9,17},{17,25},{25,1},{2,10},{10... | collective-permute-start | bytes 393224 | tf_op jit(solution)/shard_map/ppermute | solution.py:377
  47.0 1.0 %collective-permute-done.12 = f32[256,128]{1,0:T(8,128)S(1)} collective-permute-done((f32[256,128]{1,0:T(8,128)S(1)}, f32[256,128]{1,0:T(8,128)S(1)}, u32[]{:S(2)}, u32[]{:S(2)}) %collective-permute-start.12) | collective-permute-done | bytes 131104 | tf_op jit(solution)/shard_map/ppermute | solution.py:377
  48.0 0.0 collective-permute-done.13
  48.0 0.8 %shard_map.75.refs_4_ = f32[64,8,4,128]{3,2,1,0:T(4,128)} custom-call(s32[1]{0:T(128)} %bitcast.refs_0_.place, f32[64,4,128]{2,1,0:T(4,128)S(1)} %bitcast.14, f32[64,4,128]{2,1,0:T(4,128)S(1)} %bitcast.15, f32[64,4,128]{2,1,0:T(4,128)S(1)} %bitcast.16, f32[64,4,128]{2,1,0:T(4,128)S(1)} %bitcast.18), custom_call_target="tpu_custom_call" | custom-call | tf_op jit(solution)/shard_map/pallas_call | solution.py:354
  48.8 0.2 collective-permute-done.5
  49.0 7.7 %collective-permute-done.6 = f32[256,128]{1,0:T(8,128)S(1)} collective-permute-done((f32[256,128]{1,0:T(8,128)S(1)}, f32[256,128]{1,0:T(8,128)S(1)}, u32[]{:S(2)}, u32[]{:S(2)}) %collective-permute-start.6) | collective-permute-done | bytes 131104 | tf_op jit(solution)/shard_map/ppermute | solution.py:377
  56.8 0.0 collective-permute-done.7
  56.8 0.8 %shard_map.76 = f32[64,8,4,128]{3,2,1,0:T(4,128)} custom-call(s32[1]{0:T(128)} %bitcast.refs_0_.place, f32[64,4,128]{2,1,0:T(4,128)S(1)} %bitcast.17, f32[64,4,128]{2,1,0:T(4,128)S(1)} %bitcast.19, f32[64,4,128]{2,1,0:T(4,128)S(1)} %bitcast.20, f32[64,4,128]{2,1,0:T(4,128)S(1)} %bitcast.21, ...), custom_call_target="tpu_custom_call", output_to_operand_aliasing={{}: (5, {})} | custom-call | tf_op jit(solution)/shard_map/pallas_call | solution.py:354
Async XLA Ops:
  0.0 17.3 %copy-start = (f32[64,32,128]{2,1,0:T(8,128)S(1)}, f32[64,32,128]{2,1,0:T(8,128)}, u32[]{:S(2)}) copy-start(f32[64,32,128]{2,1,0:T(8,128)} %refs_2_.3) | copy-start | bytes 3145732
  4.1 13.2 %collective-permute-start = (f32[4,72,128]{2,1,0:T(8,128)S(1)}, f32[4,72,128]{2,1,0:T(8,128)S(1)}, u32[]{:S(2)}, u32[]{:S(2)}) collective-permute-start(f32[4,72,128]{2,1,0:T(8,128)S(1)} %get-tuple-element.29), channel_id=1, source_target_pairs={{0,1},{1,2},{2,3},{3,4},{4,5},{5,6},{6,7},{7,0},{8,9},{9,10},{10,1... | collective-permute-start | bytes 442376 | tf_op jit(solution)/shard_map/ppermute | solution.py:393
  4.7 12.7 %collective-permute-start.1 = (f32[4,72,128]{2,1,0:T(8,128)S(1)}, f32[4,72,128]{2,1,0:T(8,128)S(1)}, u32[]{:S(2)}, u32[]{:S(2)}) collective-permute-start(f32[4,72,128]{2,1,0:T(8,128)S(1)} %get-tuple-element.30), channel_id=1, source_target_pairs={{1,0},{2,1},{3,2},{4,3},{5,4},{6,5},{7,6},{0,7},{9,8},{10,9},{11,1... | collective-permute-start | bytes 442376 | tf_op jit(solution)/shard_map/ppermute | solution.py:394
  7.6 11.9 %collective-permute-start.8 = (f32[4,64,128]{2,1,0:T(8,128)S(1)}, f32[4,64,128]{2,1,0:T(8,128)S(1)}, u32[]{:S(2)}, u32[]{:S(2)}) collective-permute-start(f32[4,64,128]{2,1,0:T(8,128)S(1)} %get-tuple-element.44), channel_id=1, source_target_pairs={{0,8},{8,16},{16,24},{24,0},{1,9},{9,17},{17,25},{25,1},{2,10},{10... | collective-permute-start | bytes 393224 | tf_op jit(solution)/shard_map/ppermute | solution.py:377
  9.9 12.5 %collective-permute-start.9 = (f32[4,64,128]{2,1,0:T(8,128)S(1)}, f32[4,64,128]{2,1,0:T(8,128)S(1)}, u32[]{:S(2)}, u32[]{:S(2)}) collective-permute-start(f32[4,64,128]{2,1,0:T(8,128)S(1)} %get-tuple-element.45), channel_id=1, source_target_pairs={{0,16},{8,24},{16,0},{24,8},{1,17},{9,25},{17,1},{25,9},{2,18},{10... | collective-permute-start | bytes 393224 | tf_op jit(solution)/shard_map/ppermute | solution.py:377
  12.5 9.9 %collective-permute-start.10 = (f32[4,64,128]{2,1,0:T(8,128)S(1)}, f32[4,64,128]{2,1,0:T(8,128)S(1)}, u32[]{:S(2)}, u32[]{:S(2)}) collective-permute-start(f32[4,64,128]{2,1,0:T(8,128)S(1)} %get-tuple-element.46), channel_id=1, source_target_pairs={{0,24},{8,0},{16,8},{24,16},{1,25},{9,1},{17,9},{25,17},{2,26},{10... | collective-permute-start | bytes 393224 | tf_op jit(solution)/shard_map/ppermute | solution.py:377
  13.8 3.5 %copy-start.1 = (f32[2,32,128]{2,1,0:T(8,128)S(1)}, f32[2,32,128]{2,1,0:T(8,128)}, u32[]{:S(2)}) copy-start(f32[2,32,128]{2,1,0:T(8,128)} %refs_4_.1) | copy-start | bytes 98308
  13.8 3.5 %copy-start.2 = (f32[32,128]{1,0:T(8,128)S(1)}, f32[32,128]{1,0:T(8,128)}, u32[]{:S(2)}) copy-start(f32[32,128]{1,0:T(8,128)} %refs_3_.3) | copy-start | bytes 49156
  13.8 8.5 %all-to-all-start = ((f32[8,2,8,128]{3,2,1,0:T(8,128)}), f32[8,2,8,128]{3,2,1,0:T(8,128)S(1)}, u32[]{:S(2)}, u32[]{:S(2)}) async-start(f32[8,2,8,128]{3,2,1,0:T(8,128)} %get-tuple-element.28), calls=%async_computation | async-start | bytes 131072 | tf_op jit(solution)/shard_map/all_to_all | solution.py:395
  18.5 11.0 %collective-permute-start.2 = (f32[4,64,128]{2,1,0:T(8,128)S(1)}, f32[4,64,128]{2,1,0:T(8,128)S(1)}, u32[]{:S(2)}, u32[]{:S(2)}) collective-permute-start(f32[4,64,128]{2,1,0:T(8,128)S(1)} %get-tuple-element.36), channel_id=1, source_target_pairs={{0,8},{8,16},{16,24},{24,0},{1,9},{9,17},{17,25},{25,1},{2,10},{10... | collective-permute-start | bytes 393224 | tf_op jit(solution)/shard_map/ppermute | solution.py:377
  19.2 17.9 %collective-permute-start.3 = (f32[4,64,128]{2,1,0:T(8,128)S(1)}, f32[4,64,128]{2,1,0:T(8,128)S(1)}, u32[]{:S(2)}, u32[]{:S(2)}) collective-permute-start(f32[4,64,128]{2,1,0:T(8,128)S(1)} %get-tuple-element.37), channel_id=1, source_target_pairs={{0,16},{8,24},{16,0},{24,8},{1,17},{9,25},{17,1},{25,9},{2,18},{10... | collective-permute-start | bytes 393224 | tf_op jit(solution)/shard_map/ppermute | solution.py:377
  19.5 17.6 %collective-permute-start.4 = (f32[4,64,128]{2,1,0:T(8,128)S(1)}, f32[4,64,128]{2,1,0:T(8,128)S(1)}, u32[]{:S(2)}, u32[]{:S(2)}) collective-permute-start(f32[4,64,128]{2,1,0:T(8,128)S(1)} %get-tuple-element.38), channel_id=1, source_target_pairs={{0,24},{8,0},{16,8},{24,16},{1,25},{9,1},{17,9},{25,17},{2,26},{10... | collective-permute-start | bytes 393224 | tf_op jit(solution)/shard_map/ppermute | solution.py:377
  25.7 20.6 %collective-permute-start.11 = (f32[256,128]{1,0:T(8,128)S(1)}, f32[256,128]{1,0:T(8,128)S(1)}, u32[]{:S(2)}, u32[]{:S(2)}) collective-permute-start(f32[256,128]{1,0:T(8,128)S(1)} %get-tuple-element.48), channel_id=1, source_target_pairs={{0,24},{8,0},{16,8},{24,16},{1,25},{9,1},{17,9},{25,17},{2,26},{10... | collective-permute-start | bytes 393224 | tf_op jit(solution)/shard_map/ppermute | solution.py:377
  29.5 18.5 %collective-permute-start.12 = (f32[256,128]{1,0:T(8,128)S(1)}, f32[256,128]{1,0:T(8,128)S(1)}, u32[]{:S(2)}, u32[]{:S(2)}) collective-permute-start(f32[256,128]{1,0:T(8,128)S(1)} %get-tuple-element.49), channel_id=1, source_target_pairs={{0,16},{8,24},{16,0},{24,8},{1,17},{9,25},{17,1},{25,9},{2,18},{10... | collective-permute-start | bytes 393224 | tf_op jit(solution)/shard_map/ppermute | solution.py:377
  29.5 18.5 %collective-permute-start.13 = (f32[256,128]{1,0:T(8,128)S(1)}, f32[256,128]{1,0:T(8,128)S(1)}, u32[]{:S(2)}, u32[]{:S(2)}) collective-permute-start(f32[256,128]{1,0:T(8,128)S(1)} %get-tuple-element.50), channel_id=1, source_target_pairs={{0,8},{8,16},{16,24},{24,0},{1,9},{9,17},{17,25},{25,1},{2,10},{10... | collective-permute-start | bytes 393224 | tf_op jit(solution)/shard_map/ppermute | solution.py:377
  40.4 8.6 %collective-permute-start.5 = (f32[256,128]{1,0:T(8,128)S(1)}, f32[256,128]{1,0:T(8,128)S(1)}, u32[]{:S(2)}, u32[]{:S(2)}) collective-permute-start(f32[256,128]{1,0:T(8,128)S(1)} %get-tuple-element.40), channel_id=1, source_target_pairs={{0,24},{8,0},{16,8},{24,16},{1,25},{9,1},{17,9},{25,17},{2,26},{10... | collective-permute-start | bytes 393224 | tf_op jit(solution)/shard_map/ppermute | solution.py:377
  46.3 10.5 %collective-permute-start.6 = (f32[256,128]{1,0:T(8,128)S(1)}, f32[256,128]{1,0:T(8,128)S(1)}, u32[]{:S(2)}, u32[]{:S(2)}) collective-permute-start(f32[256,128]{1,0:T(8,128)S(1)} %get-tuple-element.41), channel_id=1, source_target_pairs={{0,16},{8,24},{16,0},{24,8},{1,17},{9,25},{17,1},{25,9},{2,18},{10... | collective-permute-start | bytes 393224 | tf_op jit(solution)/shard_map/ppermute | solution.py:377
  46.3 10.5 %collective-permute-start.7 = (f32[256,128]{1,0:T(8,128)S(1)}, f32[256,128]{1,0:T(8,128)S(1)}, u32[]{:S(2)}, u32[]{:S(2)}) collective-permute-start(f32[256,128]{1,0:T(8,128)S(1)} %get-tuple-element.42), channel_id=1, source_target_pairs={{0,8},{8,16},{16,24},{24,0},{1,9},{9,17},{17,25},{25,1},{2,10},{10... | collective-permute-start | bytes 393224 | tf_op jit(solution)/shard_map/ppermute | solution.py:377
